TPU v7x, 256 devices: a whole 4x4x8 slice. The times are simulated.
256 devices in a mesh: echo: 8 (over x, y_lo), coil: 16 (over z, core), read: 2 (over y_hi).
Axes of the slice: x: 4, y: 4 (y_hi: 2, y_lo: 2; y = y_hi * 2 + y_lo), z: 8, core: 2. Of those that a mesh axis runs over, the one named last changes fastest.
Arguments:
- kspace: bfloat16 [384, 8, 16, 4, 2, 192], P(None, 'echo', 'coil', 'read'), may hold values from -3 to 3
- sampling: int32 [384, 8, 192], P(None, 'echo'), may hold values 0 or 1
- coil_maps: bfloat16 [384, 16, 4, 2, 192], P(None, 'coil', 'read'), may hold values from -1.5 to 1.5
- image: float32 [384, 8, 4, 2, 192], P('coil', 'echo', 'read'), may hold values from -6 to 6
- filters: bfloat16 [48, 3, 3, 3, 2], replicated, may hold values from -0.875 to 0.875
- thresholds: float32 [48], replicated, may hold values from 0.5 to 8
- dc_weight: float32 [8], P('echo'), may hold values from 0.5 to 2
Outputs:
- updated: float32 [384, 8, 4, 2, 192], P('coil', 'echo', 'read')
All inputs are finite; a program needn't handle non-finite values. No bound on the sum of `sampling` on one device may be relied on, other than what follows from the above.
Results may differ from a plain program's by a relative error of at most 0.0033.
Values may be sent and summed in bfloat16 or wider, within the bound.
No kernel may reach another device: no remote copies, remote signals or barrier semaphores. Data moves between devices by JAX's collectives and lax.ppermute only.
A program may use at most 128 MiB of HBM per device.

v0:
```python
import jax
import jax.numpy as jnp
from jax import lax
from jax.sharding import PartitionSpec as P

NY = 384
NZ = 192


def in_order(parts, dim):
    shape = list(parts.shape[1:])
    shape[dim] *= parts.shape[0]
    return jnp.moveaxis(parts, 0, dim).reshape(shape)


def from_everyone(array, axis):
    copies = jnp.broadcast_to(array, (lax.axis_size(axis), *array.shape))
    return lax.all_to_all(copies, axis, split_axis=0, concat_axis=0, tiled=True)


def gathered_copies(array, axis, dim):
    return in_order(from_everyone(array, axis), dim)


def cut_along(array, dim, length):
    shape = array.shape
    parts = array.reshape(*shape[:dim], length, shape[dim] // length, *shape[dim + 1 :])
    return jnp.moveaxis(parts, dim, 0)


def summed_on_arrival(array, axis, dim):
    length = lax.axis_size(axis)
    parts = lax.all_to_all(cut_along(array, dim, length), axis, 0, 0, tiled=True)
    return jnp.sum(parts.astype(jnp.float32), axis=0)


def extended(block, sides, width):
    for axis, dim in sides:
        count = lax.axis_size(axis)
        forward = [(i, i + 1) for i in range(count - 1)]
        backward = [(target, source) for source, target in forward]
        low = lax.ppermute(
            lax.slice_in_dim(block, block.shape[dim] - width, None, axis=dim), axis, forward
        )
        high = lax.ppermute(lax.slice_in_dim(block, 0, width, axis=dim), axis, backward)
        block = jnp.concatenate([low, block, high], axis=dim)
    return block


def tables(length):
    positions = jnp.arange(length, dtype=jnp.int32)
    product = positions[:, None] * positions[None, :] % length
    phases = product.astype(jnp.float32) * (2.0 * jnp.pi / length)
    normalize = length ** (-0.5)
    return (jnp.cos(phases) * normalize, jnp.sin(phases) * normalize)


def complex_times(left, right, conjugate):
    left_real = left[..., 0, :]
    left_imag = left[..., 1, :]
    right_real = right[..., 0, :]
    right_imag = right[..., 1, :]
    if conjugate:
        return jnp.stack(
            [
                left_real * right_real + left_imag * right_imag,
                left_real * right_imag - left_imag * right_real,
            ],
            -2,
        )
    return jnp.stack(
        [
            left_real * right_real - left_imag * right_imag,
            left_real * right_imag + left_imag * right_real,
        ],
        -2,
    )


def column_section(values, block):
    shape = values.shape
    merged = values.reshape(shape[:-2] + (shape[-2] * shape[-1],))
    result = jnp.dot(merged, block, preferred_element_type=jnp.float32)
    return result.reshape(shape)


def row_section(values, row_table, adjoint):
    lines = values.shape[0]
    result = jnp.einsum("ay,y...->a...", row_table, values, preferred_element_type=jnp.float32)
    cosine_part = result[:lines]
    sine_part = result[lines:]
    if adjoint:
        return jnp.stack(
            [
                cosine_part[..., 0, :] - sine_part[..., 1, :],
                cosine_part[..., 1, :] + sine_part[..., 0, :],
            ],
            -2,
        )
    return jnp.stack(
        [
            cosine_part[..., 0, :] + sine_part[..., 1, :],
            cosine_part[..., 1, :] - sine_part[..., 0, :],
        ],
        -2,
    )


def coil_side(halfway, kspace, sampling, row_table):
    sampled = sampling.astype(jnp.float32)[:, :, None, None, None, :]
    spectrum = row_section(halfway, row_table, False)
    residual = (sampled * (spectrum - kspace.astype(jnp.float32))).astype(jnp.bfloat16)
    return row_section(residual, row_table, True).astype(jnp.bfloat16)


def respond(padded, weights, row_count, slices):
    columns = padded.shape[-1]
    z_padded = jnp.pad(padded, ((0, 0), (0, 0), (0, 0), (0, 0), (1, 1)))
    patches = jnp.stack(
        [
            z_padded[
                shift_y : shift_y + row_count,
                :,
                shift_r : shift_r + slices,
                :,
                shift_z : shift_z + columns,
            ]
            for shift_y in range(3)
            for shift_r in range(3)
            for shift_z in range(3)
        ],
        0,
    )
    return jnp.einsum("koc,oyercz->kyerz", weights, patches, preferred_element_type=jnp.float32)


def shrink(response, energy, thresholds):
    magnitude = jnp.sqrt(energy)
    factor = magnitude / (magnitude + thresholds[:, None, None, None])
    return (response * factor[:, :, None]).astype(jnp.bfloat16)


def transposed(shrunk_pad, weights, row_count, slices):
    columns = shrunk_pad.shape[-1]
    z_padded = jnp.pad(shrunk_pad, ((0, 0), (0, 0), (0, 0), (0, 0), (1, 1)))
    summed = jnp.zeros((row_count, z_padded.shape[2], slices, 2, columns), jnp.float32)
    for shift_y in range(3):
        for shift_r in range(3):
            for shift_z in range(3):
                offset = shift_y * 9 + shift_r * 3 + shift_z
                window = z_padded[
                    :,
                    2 - shift_y : 2 - shift_y + row_count,
                    :,
                    2 - shift_r : 2 - shift_r + slices,
                    2 - shift_z : 2 - shift_z + columns,
                ]
                summed = summed + jnp.einsum(
                    "kc,kyerz->yercz",
                    weights[:, offset],
                    window,
                    preferred_element_type=jnp.float32,
                )
    return summed


def body(kspace, sampling, coil_maps, image, filters, thresholds, dc_weight):
    row_cos, row_sin = tables(NY)
    row_table = jnp.concatenate([row_cos, row_sin], 0).astype(jnp.bfloat16)
    col_cos, col_sin = tables(NZ)
    forward_block = jnp.block([[col_cos, -col_sin], [col_sin, col_cos]]).astype(jnp.bfloat16)
    adjoint_block = jnp.block([[col_cos, col_sin], [-col_sin, col_cos]]).astype(jnp.bfloat16)
    rounded = image.astype(jnp.bfloat16)
    row_count = image.shape[0]
    slices = image.shape[2]
    gathered = gathered_copies(rounded, "coil", 0)
    sensitivity = coil_maps[:, 0]
    weighted = complex_times(
        sensitivity[:, None].astype(jnp.float32), gathered.astype(jnp.float32), False
    ).astype(jnp.bfloat16)
    halfway = column_section(weighted[:, :, None], forward_block).astype(jnp.bfloat16)
    backward = coil_side(halfway, kspace, sampling, row_table)[:, :, 0]
    restored = column_section(backward, adjoint_block)
    adjoint = summed_on_arrival(
        complex_times(sensitivity[:, None].astype(jnp.float32), restored, True).astype(
            jnp.bfloat16
        ),
        "coil",
        0,
    )
    weights = filters.reshape(filters.shape[0], 27, 2)
    padded = extended(rounded, (("coil", 0), ("read", 2)), 1)
    response = respond(padded, weights, row_count, slices)
    energy = lax.psum(jnp.sum(response * response, axis=2).astype(jnp.bfloat16), "echo").astype(
        jnp.float32
    )
    shrunk = shrink(response, energy, thresholds)
    shrunk_pad = extended(shrunk, (("coil", 1), ("read", 3)), 1)
    penalty = transposed(shrunk_pad, weights, row_count, slices)
    return image - dc_weight[None, :, None, None, None] * adjoint - penalty


def solution(mesh):
    return jax.shard_map(
        body,
        mesh=mesh,
        in_specs=(
            P(None, "echo", "coil", "read", None, None),
            P(None, "echo", None),
            P(None, "coil", "read", None, None),
            P("coil", "echo", "read", None, None),
            P(),
            P(),
            P("echo"),
        ),
        out_specs=P("coil", "echo", "read", None, None),
        check_vma=False,
    )
```

profile of v0, /device:TPU:17, one launch (start us, length us, event | category | flops | bytes accessed | tf_op | source)
XLA Modules:
  0.0 206.4 jit_solution(4025107050509815541)
XLA Ops:
  6.5 0.9 copy.1479
  7.5 4.1 %collective-permute-start = (bf16[1,1,2,2,192]{4,0,3,2,1:T(2,128)(2,1)S(1)}, bf16[1,1,2,2,192]{4,0,3,2,1:T(2,128)(2,1)S(1)}, u32[]{:S(2)}, u32[]{:S(2)}) collective-permute-start(bf16[1,1,2,2,192]{4,0,3,2,1:T(2,128)(2,1)S(1)} %get-tuple-element.57), channel_id=1, source_target_pairs={{0,2},{2,4},{4,6},{6,8},{8,10},{10,12},{12,14},{14,16},{16,18},{18... | collective-permute-start | bytes 4616 | tf_op jit(solution)/shard_map/ppermute | solution.py:42
  11.6 1.9 collective-permute-start.1
  13.5 0.9 copy.1485
  14.5 2.0 collective-permute-done.1
  16.6 1.3 collective-permute-start.2
  17.9 5.5 %collective-permute-start.3 = (bf16[26,1,1,2,192]{4,0,3,2,1:T(8,128)(2,1)S(1)}, bf16[26,1,1,2,192]{4,0,3,2,1:T(8,128)(2,1)S(1)}, u32[]{:S(2)}, u32[]{:S(2)}) collective-permute-start(bf16[26,1,1,2,192]{4,0,3,2,1:T(8,128)(2,1)S(1)} %get-tuple-element.52), channel_id=1, source_target_pairs={{1,0},{3,2},{5,4},{7,6},{9,8},{11,10},{13,12},{15,14},{17,16},{19,... | collective-permute-start | bytes 59912 | tf_op jit(solution)/shard_map/ppermute | solution.py:45
  23.6 0.8 collective-permute-done.3
  26.3 0.7 copy.1418
  27.0 0.7 copy.1419
  27.7 0.7 copy.1421
  28.4 0.7 copy.1422
  29.2 0.7 copy.1424
  29.9 0.7 copy.1425
  31.3 6.7 %stack.141 = bf16[27,24,1,2,2,192]{5,0,4,3,1,2:T(8,128)(2,1)S(1)} concatenate(bf16[1,24,1,2,2,192]{5,0,4,3,1,2:T(2,128)(2,1)S(1)} %copy.1401, bf16[1,24,1,2,2,192]{5,0,4,3,1,2:T(2,128)(2,1)S(1)} %copy.1402, bf16[1,24,1,2,2,192]{5,0,4,3,1,2:T(2,128)(2,1)S(1)} %copy.1403, bf16[1,24,1,2,2,192]{5,0,4,3,1,2:T(2,128)(2,1)S(1)} %copy.1404, bf16[1,24,1,2,2,192]{5,0,4,3,1,2:T(2,128)(2,1)S(1)} %copy.1405, ...), dimensions={0} | concatenate | bytes 1990656 | tf_op jit(solution)/shard_map/stack | solution.py:119
  38.0 2.4 %fusion.8 = (bf16[48,24,2,192]{3,0,2,1:T(8,128)(2,1)}, f32[24,2,192,48,1]{2,3,4,1,0:T(8,128)}) fusion(bf16[48,27,2,1,1]{0,2,1,4,3:T(2,128)(2,1)S(1)} %bitcast.601, bf16[27,24,1,2,2,192]{5,0,4,3,1,2:T(8,128)(2,1)S(1)} %stack.141), kind=kOutput, calls=%fused_computation.14 | convolution fusion | flops 48660480 | bytes 3654720 | tf_op jit(solution)/shard_map/koc,oyercz->kyerz/dot_general | solution.py:134
  40.4 1.0 broadcast_in_dim.2
  41.5 9.3 %all-to-all-start = ((bf16[16,24,1,2,2,192]{5,1,4,3,2,0:T(8,128)(2,1)}), bf16[16,24,1,2,2,192]{5,1,4,3,2,0:T(8,128)(2,1)S(1)}, u32[]{:S(2)}, u32[]{:S(2)}) async-start(bf16[16,24,1,2,2,192]{5,1,4,3,2,0:T(8,128)(2,1)} %broadcast_in_dim.2), calls=%async_computation | async-start | bytes 1572864 | tf_op jit(solution)/shard_map/all_to_all | solution.py:18
  51.6 0.8 fusion.105
  52.4 0.8 negate_convert_fusion
  53.2 3.2 %multiply_convert_fusion = (bf16[384,384]{1,0:T(8,128)(2,1)S(1)}, bf16[384,384]{1,0:T(8,128)(2,1)}) fusion(), kind=kLoop, calls=%fused_computation.144 | loop fusion | flops 1916928 | bytes 589824 | tf_op jit(solution)/shard_map/convert.22
  56.4 1.0 fusion.98
  57.4 0.7 convert_bitcast_fusion
  58.2 66.2 %all-reduce.4.cloned.1.call-done = bf16[48,24,2,192]{3,0,2,1:T(8,128)(2,1)} async-done(((bf16[48,24,2,192]{3,0,2,1:T(8,128)(2,1)}), bf16[48,24,2,192]{3,0,2,1:T(8,128)(2,1)}) %all-reduce.4.cloned.1.call-update) | async-done | bytes 884752 | tf_op jit(solution)/shard_map/psum | solution.py:194
  124.4 3.0 %fusion.7 = bf16[48,24,2,192]{3,0,2,1:T(8,128)(2,1)S(1)} fusion(f32[24,2,192,48,1]{2,3,4,1,0:T(8,128)} %get-tuple-element.60, bf16[48,24,2,192]{3,0,2,1:T(8,128)(2,1)} %all-reduce.4.cloned.1.call-done, f32[48]{0:T(128)} %param.12), kind=kLoop, calls=%fused_computation.12 | loop fusion | flops 2211840 | bytes 3539136 | tf_op jit(solution)/shard_map/convert_element_type | solution.py:140
  127.4 6.8 %collective-permute-start.5 = (bf16[48,1,1,2,192]{4,0,3,1,2:T(8,128)(2,1)S(1)}, bf16[48,1,1,2,192]{4,0,3,1,2:T(8,128)(2,1)S(1)}, u32[]{:S(2)}, u32[]{:S(2)}) collective-permute-start(bf16[48,1,1,2,192]{4,0,3,1,2:T(8,128)(2,1)S(1)} %get-tuple-element.24), channel_id=1, source_target_pairs={{2,0},{4,2},{6,4},{8,6},{10,8},{12,10},{14,12},{16,14},{18,16},{20... | collective-permute-start | bytes 110600 | tf_op jit(solution)/shard_map/ppermute | solution.py:45
  134.2 3.1 %collective-permute-start.4 = (bf16[48,1,1,2,192]{4,0,3,1,2:T(8,128)(2,1)S(1)}, bf16[48,1,1,2,192]{4,0,3,1,2:T(8,128)(2,1)S(1)}, u32[]{:S(2)}, u32[]{:S(2)}) collective-permute-start(bf16[48,1,1,2,192]{4,0,3,1,2:T(8,128)(2,1)S(1)} %get-tuple-element.23), channel_id=1, source_target_pairs={{0,2},{2,4},{4,6},{6,8},{8,10},{10,12},{12,14},{14,16},{16,18},{18... | collective-permute-start | bytes 110600 | tf_op jit(solution)/shard_map/ppermute | solution.py:42
  137.3 0.9 fusion.115
  138.7 1.1 fusion.121
  139.8 1.3 collective-permute-start.6
  141.1 7.1 %collective-permute-start.7 = (bf16[48,26,1,1,192]{4,0,3,1,2:T(8,128)(2,1)}, bf16[48,26,1,1,192]{4,0,3,1,2:T(8,128)(2,1)}, u32[]{:S(2)}, u32[]{:S(2)}) collective-permute-start(bf16[48,26,1,1,192]{4,0,3,1,2:T(8,128)(2,1)} %get-tuple-element.22), channel_id=1, source_target_pairs={{1,0},{3,2},{5,4},{7,6},{9,8},{11,10},{13,12},{15,14},{17,16},{19,... | collective-permute-start | bytes 1437704 | tf_op jit(solution)/shard_map/ppermute | solution.py:45
  148.2 1.1 fusion.58
  149.3 1.0 fusion.36
  150.5 1.0 fusion.120
  151.5 2.2 %copy.1468 = f32[384,1,2,1,192]{0,4,3,2,1:T(8,128)} copy(f32[384,1,2,1,192]{4,0,3,2,1:T(8,128)} %get-tuple-element.18) | data formatting | bytes 1179648
  153.8 1.1 copy.1469
  154.8 1.4 subtract_convert_fusion.1
  156.3 0.9 copy-done.3
  157.7 0.8 fusion.96
  158.8 0.8 copy-done.4
  160.0 0.8 fusion.95
  161.2 0.9 copy-done.2
  163.3 1.0 copy.1397
  164.3 10.0 %all-to-all-start.1 = ((bf16[16,24,1,2,2,192]{5,1,3,4,2,0:T(8,128)(2,1)}), bf16[16,24,1,2,2,192]{5,1,3,4,2,0:T(8,128)(2,1)S(1)}, u32[]{:S(2)}, u32[]{:S(2)}) async-start(bf16[16,24,1,2,2,192]{5,1,3,4,2,0:T(8,128)(2,1)} %copy.1397), calls=%async_computation.1 | async-start | bytes 1572864 | tf_op jit(solution)/shard_map/all_to_all | solution.py:33
  174.3 1.9 pad_maximum_fusion
  176.8 3.5 %select_maximum_fusion = bf16[48,26,1,4,194]{4,0,3,1,2:T(8,128)(2,1)S(1)} fusion(bf16[48,26,1,1,192]{4,0,3,1,2:T(8,128)(2,1)} %collective-permute-done.7, bf16[48,26,1,1,192]{4,0,3,1,2:T(8,128)(2,1)} %collective-permute-done.6, bf16[48,1,1,2,192]{4,0,3,1,2:T(8,128)(2,1)S(1)} %copy-done.9, bf16[48,24,1,2,192]{4,0,3,1,2:T(8,128)(2,1)S(1)} %bitcast.587, ...), kind=kLoop, calls=%fused_computation.4 | loop fusion | flops 17432064 | bytes 3853824 | tf_op jit(solution)/shard_map/concatenate | solution.py:46
  188.4 8.6 %all-to-all-done.1 = bf16[16,24,1,2,2,192]{5,1,3,4,2,0:T(8,128)(2,1)S(1)} async-done(((bf16[16,24,1,2,2,192]{5,1,3,4,2,0:T(8,128)(2,1)}), bf16[16,24,1,2,2,192]{5,1,3,4,2,0:T(8,128)(2,1)S(1)}, u32[]{:S(2)}, u32[]{:S(2)}) %all-to-all-start.1) | async-done | bytes 589856 | tf_op jit(solution)/shard_map/all_to_all | solution.py:33
  197.1 2.4 %fusion.87 = f32[24,1,2,2,192]{4,3,2,1,0:T(2,128)} fusion(f32[24,1,2,2,192]{4,3,2,0,1:T(2,128)S(1)} %fusion.64, f32[24,1,2,2,192]{4,3,2,0,1:T(2,128)S(1)} %fusion.63, f32[24,1,2,2,192]{4,3,2,0,1:T(2,128)S(1)} %fusion.62, f32[24,1,2,2,192]{4,3,2,0,1:T(2,128)S(1)} %fusion.61, f32[24,1,2,2,192]{4,3,2,0,1:T(2,128)S(1)} %copy-done.15, ...), kind=kOutput, calls=%fused_computation.126 | convolution fusion | flops 2045952 | bytes 2728448 | tf_op jit(solution)/shard_map/kc,kyerz->yercz/dot_general | solution.py:158
  (112 shorter events, 15.1 us)
Async XLA Ops:
  6.5 117.8 %all-reduce.4.cloned.1.call-start = ((), (), s32[]{:S(2)}) async-start(), calls=%async_computation.2 | async-start | bytes 2359296 | tf_op jit(solution)/shard_map/psum | solution.py:194
  7.5 7.0 %collective-permute-start = (bf16[1,1,2,2,192]{4,0,3,2,1:T(2,128)(2,1)S(1)}, bf16[1,1,2,2,192]{4,0,3,2,1:T(2,128)(2,1)S(1)}, u32[]{:S(2)}, u32[]{:S(2)}) collective-permute-start(bf16[1,1,2,2,192]{4,0,3,2,1:T(2,128)(2,1)S(1)} %get-tuple-element.57), channel_id=1, source_target_pairs={{0,2},{2,4},{4,6},{6,8},{8,10},{10,12},{12,14},{14,16},{16,18},{18... | collective-permute-start | bytes 4616 | tf_op jit(solution)/shard_map/ppermute | solution.py:42
  11.6 4.9 %collective-permute-start.1 = (bf16[1,1,2,2,192]{4,0,3,2,1:T(2,128)(2,1)S(1)}, bf16[1,1,2,2,192]{4,0,3,2,1:T(2,128)(2,1)S(1)}, u32[]{:S(2)}, u32[]{:S(2)}) collective-permute-start(bf16[1,1,2,2,192]{4,0,3,2,1:T(2,128)(2,1)S(1)} %get-tuple-element.58), channel_id=1, source_target_pairs={{2,0},{4,2},{6,4},{8,6},{10,8},{12,10},{14,12},{16,14},{18,16},{20... | collective-permute-start | bytes 4616 | tf_op jit(solution)/shard_map/ppermute | solution.py:45
  16.6 7.0 %collective-permute-start.2 = (bf16[26,1,1,2,192]{4,0,3,2,1:T(8,128)(2,1)S(1)}, bf16[26,1,1,2,192]{4,0,3,2,1:T(8,128)(2,1)S(1)}, u32[]{:S(2)}, u32[]{:S(2)}) collective-permute-start(bf16[26,1,1,2,192]{4,0,3,2,1:T(8,128)(2,1)S(1)} %get-tuple-element.51), channel_id=1, source_target_pairs={{0,1},{2,3},{4,5},{6,7},{8,9},{10,11},{12,13},{14,15},{16,17},{18,... | collective-permute-start | bytes 59912 | tf_op jit(solution)/shard_map/ppermute | solution.py:42
  17.9 6.5 %collective-permute-start.3 = (bf16[26,1,1,2,192]{4,0,3,2,1:T(8,128)(2,1)S(1)}, bf16[26,1,1,2,192]{4,0,3,2,1:T(8,128)(2,1)S(1)}, u32[]{:S(2)}, u32[]{:S(2)}) collective-permute-start(bf16[26,1,1,2,192]{4,0,3,2,1:T(8,128)(2,1)S(1)} %get-tuple-element.52), channel_id=1, source_target_pairs={{1,0},{3,2},{5,4},{7,6},{9,8},{11,10},{13,12},{15,14},{17,16},{19,... | collective-permute-start | bytes 59912 | tf_op jit(solution)/shard_map/ppermute | solution.py:45
  31.3 6.7 %copy-start.14 = (bf16[48,3,3,3,2]{0,4,3,2,1:T(2,128)(2,1)S(1)}, bf16[48,3,3,3,2]{0,4,3,2,1:T(2,128)(2,1)}, u32[]{:S(2)}) copy-start(bf16[48,3,3,3,2]{0,4,3,2,1:T(2,128)(2,1)} %param.11) | copy-start | bytes 15556
  38.0 2.4 %copy-start.5 = (f32[24,1,2,2,192]{4,3,2,1,0:T(2,128)S(1)}, f32[24,1,2,2,192]{4,3,2,1,0:T(2,128)}, u32[]{:S(2)}) copy-start(f32[24,1,2,2,192]{4,3,2,1,0:T(2,128)} %param.10) | copy-start | bytes 221188
  40.4 10.4 %copy-start.6 = (bf16[384,1,2,2,192]{0,4,3,2,1:T(8,128)(2,1)S(1)}, bf16[384,1,2,2,192]{0,4,3,2,1:T(8,128)(2,1)}, u32[]{:S(2)}) copy-start(bf16[384,1,2,2,192]{0,4,3,2,1:T(8,128)(2,1)} %param.9) | copy-start | bytes 1769476
  41.5 108.9 %all-to-all-start = ((bf16[16,24,1,2,2,192]{5,1,4,3,2,0:T(8,128)(2,1)}), bf16[16,24,1,2,2,192]{5,1,4,3,2,0:T(8,128)(2,1)S(1)}, u32[]{:S(2)}, u32[]{:S(2)}) async-start(bf16[16,24,1,2,2,192]{5,1,4,3,2,0:T(8,128)(2,1)} %broadcast_in_dim.2), calls=%async_computation | async-start | bytes 1572864 | tf_op jit(solution)/shard_map/all_to_all | solution.py:18
  50.9 6.6 %copy-start.12 = (s32[384,1,192]{0,2,1:T(8,128)S(1)}, s32[384,1,192]{0,2,1:T(8,128)}, u32[]{:S(2)}) copy-start(s32[384,1,192]{0,2,1:T(8,128)} %param.8) | copy-start | bytes 884740
  127.4 10.8 %collective-permute-start.5 = (bf16[48,1,1,2,192]{4,0,3,1,2:T(8,128)(2,1)S(1)}, bf16[48,1,1,2,192]{4,0,3,1,2:T(8,128)(2,1)S(1)}, u32[]{:S(2)}, u32[]{:S(2)}) collective-permute-start(bf16[48,1,1,2,192]{4,0,3,1,2:T(8,128)(2,1)S(1)} %get-tuple-element.24), channel_id=1, source_target_pairs={{2,0},{4,2},{6,4},{8,6},{10,8},{12,10},{14,12},{16,14},{18,16},{20... | collective-permute-start | bytes 110600 | tf_op jit(solution)/shard_map/ppermute | solution.py:45
  134.2 4.2 %collective-permute-start.4 = (bf16[48,1,1,2,192]{4,0,3,1,2:T(8,128)(2,1)S(1)}, bf16[48,1,1,2,192]{4,0,3,1,2:T(8,128)(2,1)S(1)}, u32[]{:S(2)}, u32[]{:S(2)}) collective-permute-start(bf16[48,1,1,2,192]{4,0,3,1,2:T(8,128)(2,1)S(1)} %get-tuple-element.23), channel_id=1, source_target_pairs={{0,2},{2,4},{4,6},{6,8},{8,10},{10,12},{12,14},{14,16},{16,18},{18... | collective-permute-start | bytes 110600 | tf_op jit(solution)/shard_map/ppermute | solution.py:42
  138.2 11.1 %copy-start.8 = (bf16[48,1,1,2,192]{4,0,3,1,2:T(8,128)(2,1)}, bf16[48,1,1,2,192]{4,0,3,1,2:T(8,128)(2,1)S(1)}, u32[]{:S(2)}) copy-start(bf16[48,1,1,2,192]{4,0,3,1,2:T(8,128)(2,1)S(1)} %collective-permute-done.5) | copy-start | bytes 110596
  138.4 9.8 %copy-start.10 = (bf16[48,1,1,2,192]{4,0,3,1,2:T(8,128)(2,1)}, bf16[48,1,1,2,192]{4,0,3,1,2:T(8,128)(2,1)S(1)}, u32[]{:S(2)}) copy-start(bf16[48,1,1,2,192]{4,0,3,1,2:T(8,128)(2,1)S(1)} %collective-permute-done.4) | copy-start | bytes 110596
  139.8 34.5 %collective-permute-start.6 = (bf16[48,26,1,1,192]{4,0,3,1,2:T(8,128)(2,1)}, bf16[48,26,1,1,192]{4,0,3,1,2:T(8,128)(2,1)}, u32[]{:S(2)}, u32[]{:S(2)}) collective-permute-start(bf16[48,26,1,1,192]{4,0,3,1,2:T(8,128)(2,1)} %get-tuple-element.21), channel_id=1, source_target_pairs={{0,1},{2,3},{4,5},{6,7},{8,9},{10,11},{12,13},{14,15},{16,17},{18,... | collective-permute-start | bytes 1437704 | tf_op jit(solution)/shard_map/ppermute | solution.py:42
  141.1 33.2 %collective-permute-start.7 = (bf16[48,26,1,1,192]{4,0,3,1,2:T(8,128)(2,1)}, bf16[48,26,1,1,192]{4,0,3,1,2:T(8,128)(2,1)}, u32[]{:S(2)}, u32[]{:S(2)}) collective-permute-start(bf16[48,26,1,1,192]{4,0,3,1,2:T(8,128)(2,1)} %get-tuple-element.22), channel_id=1, source_target_pairs={{1,0},{3,2},{5,4},{7,6},{9,8},{11,10},{13,12},{15,14},{17,16},{19,... | collective-permute-start | bytes 1437704 | tf_op jit(solution)/shard_map/ppermute | solution.py:45
  156.2 1.0 copy-start.3
  156.2 1.4 copy-start
  158.6 1.0 copy-start.4
  158.7 1.1 copy-start.7
  161.2 1.0 copy-start.2
  163.3 11.0 %copy-start.9 = (bf16[48,1,1,2,192]{4,0,3,1,2:T(8,128)(2,1)S(1)}, bf16[48,1,1,2,192]{4,0,3,1,2:T(8,128)(2,1)}, u32[]{:S(2)}) copy-start(bf16[48,1,1,2,192]{4,0,3,1,2:T(8,128)(2,1)} %copy-done.8) | copy-start | bytes 110596
  163.3 11.0 %copy-start.11 = (bf16[48,1,1,2,192]{4,0,3,1,2:T(8,128)(2,1)S(1)}, bf16[48,1,1,2,192]{4,0,3,1,2:T(8,128)(2,1)}, u32[]{:S(2)}) copy-start(bf16[48,1,1,2,192]{4,0,3,1,2:T(8,128)(2,1)} %copy-done.10) | copy-start | bytes 110596
  164.3 32.6 %all-to-all-start.1 = ((bf16[16,24,1,2,2,192]{5,1,3,4,2,0:T(8,128)(2,1)}), bf16[16,24,1,2,2,192]{5,1,3,4,2,0:T(8,128)(2,1)S(1)}, u32[]{:S(2)}, u32[]{:S(2)}) async-start(bf16[16,24,1,2,2,192]{5,1,3,4,2,0:T(8,128)(2,1)} %copy.1397), calls=%async_computation.1 | async-start | bytes 1572864 | tf_op jit(solution)/shard_map/all_to_all | solution.py:33
  180.3 7.3 %copy-start.1 = (bf16[48,26,1,4,194]{4,0,3,1,2:T(8,128)(2,1)}, bf16[48,26,1,4,194]{4,0,3,1,2:T(8,128)(2,1)S(1)}, u32[]{:S(2)}) copy-start(bf16[48,26,1,4,194]{4,0,3,1,2:T(8,128)(2,1)S(1)} %select_maximum_fusion) | copy-start | bytes 5810692
  186.9 0.9 copy-start.13
  186.9 0.9 copy-start.16
  187.8 9.3 %copy-start.15 = (f32[24,1,2,2,192]{4,3,2,0,1:T(2,128)S(1)}, f32[24,1,2,2,192]{4,3,2,0,1:T(2,128)}, u32[]{:S(2)}) copy-start(f32[24,1,2,2,192]{4,3,2,0,1:T(2,128)} %fusion.58) | copy-start | bytes 221188
Sparse Core Ops, SparseCore 0:
  40.5 83.8 all-reduce.3
where the time goes:
time: 207 us; the launch traced here: 206 us
  waiting for transfers between devices  77.8 us (38%)
  starting transfers between devices  50.4 us (24%)
  local copies, waits for them, and re-layouts  26.6 us (13%)
  matrix products  18.7 us (9%)
  other arithmetic  18.1 us (9%)
  between operations  14.7 us (7%)
    psum x1, waiting for transfers between devices, body(): lax.psum(jnp.sum(response * response, axis=2).astype(jnp.bfloat16), 'echo')  66.2 us
    ppermute x4, starting transfers between devices, extended(): lax.ppermute(lax.slice_in_dim(block, 0, width, axis=dim), axis, backward)  21.3 us
    dot_general x27, matrix products, transposed(): jnp.einsum('kc,kyerz->yercz', weights[:, offset], window, preferred_eleme...  13.8 us
    another operation x30, local copies, waits for them, and re-layouts, respond(): jnp.stack([z_padded[shift_y:shift_y + row_count, :, shift_r:shift_r + sli...  13.5 us
    all_to_all x1, starting transfers between devices, summed_on_arrival(): lax.all_to_all(cut_along(array, dim, length), axis, 0, 0, tiled=True)  9.97 us
    ppermute x4, starting transfers between devices, extended(): lax.ppermute(lax.slice_in_dim(block, block.shape[dim] - width, None, axis...  9.76 us
    all_to_all x1, starting transfers between devices, from_everyone(): return lax.all_to_all(copies, axis, split_axis=0, concat_axis=0, tiled=True)  9.34 us
    all_to_all x1, waiting for transfers between devices, summed_on_arrival(): lax.all_to_all(cut_along(array, dim, length), axis, 0, 0, tiled=True)  8.58 us
  transfers between devices with their start and end apart: 11, of which 5 were waited for; matrix products, arithmetic and copies ran while one was open for 20% of the time, Pallas kernels for 0%

commit v1 on v0

--- a/solution.py
+++ b/solution.py
@@ -191,9 +191,9 @@
     weights = filters.reshape(filters.shape[0], 27, 2)
     padded = extended(rounded, (("coil", 0), ("read", 2)), 1)
     response = respond(padded, weights, row_count, slices)
-    energy = lax.psum(jnp.sum(response * response, axis=2).astype(jnp.bfloat16), "echo").astype(
-        jnp.float32
-    )
+    energy = jnp.sum(
+        lax.all_gather(jnp.sum(response * response, axis=2).astype(jnp.bfloat16), "echo"), axis=0
+    ).astype(jnp.float32)
     shrunk = shrink(response, energy, thresholds)
     shrunk_pad = extended(shrunk, (("coil", 1), ("read", 3)), 1)
     penalty = transposed(shrunk_pad, weights, row_count, slices)

time: 207 us -> 295 us (1.43); the launches traced: 206 us -> 289 us
  waiting for transfers between devices: 77.8 us -> 174 us
  starting transfers between devices: 50.4 us -> 34.1 us
  other arithmetic: 18.1 us -> 22.8 us
    all_gather x0 -> x1, waiting for transfers between devices: none -> 115 us  [body(): lax.all_gather(jnp.sum(response * response, axis=2).astype(jnp.bfloat16),...]
    psum x1 -> x0, waiting for transfers between devices: 66.2 us -> none  [body(): lax.psum(jnp.sum(response * response, axis=2).astype(jnp.bfloat16), 'echo')]
    all_to_all x1, waiting for transfers between devices: 0.01 us -> 14.9 us  [from_everyone(): return lax.all_to_all(copies, axis, split_axis=0, concat_axis=0, tiled=True)]
    all_to_all x1, waiting for transfers between devices: 8.58 us -> 21.7 us  [summed_on_arrival(): lax.all_to_all(cut_along(array, dim, length), axis, 0, 0, tiled=True)]
    ppermute x4, starting transfers between devices: 21.3 us -> 10 us  [extended(): lax.ppermute(lax.slice_in_dim(block, 0, width, axis=dim), axis, backward)]
    ppermute x4, waiting for transfers between devices: 0.24 us -> 11.5 us  [extended(): lax.ppermute(lax.slice_in_dim(block, block.shape[dim] - width, None, axis...]
    ppermute x4, waiting for transfers between devices: 2.77 us -> 11 us  [extended(): lax.ppermute(lax.slice_in_dim(block, 0, width, axis=dim), axis, backward)]
    all_to_all x1, starting transfers between devices: 9.97 us -> 3.51 us  [summed_on_arrival(): lax.all_to_all(cut_along(array, dim, length), axis, 0, 0, tiled=True)]
  transfers between devices with their start and end apart: 11 -> 11, of which waited for: 5 -> 7; matrix products, arithmetic and copies ran while one was open for 20% -> 10% of each run, Pallas kernels for 0% -> 0%
where the time goes in v1:
time: 295 us; the launch traced here: 289 us
  waiting for transfers between devices  174 us (59%)
  starting transfers between devices  34.1 us (12%)
  local copies, waits for them, and re-layouts  27 us (9%)
  other arithmetic  22.8 us (8%)
  matrix products  16.1 us (5%)
  between operations  14.7 us (5%)
    all_gather x1, waiting for transfers between devices, body(): lax.all_gather(jnp.sum(response * response, axis=2).astype(jnp.bfloat16),...  115 us
    all_to_all x1, waiting for transfers between devices, summed_on_arrival(): lax.all_to_all(cut_along(array, dim, length), axis, 0, 0, tiled=True)  21.7 us
    all_to_all x1, waiting for transfers between devices, from_everyone(): return lax.all_to_all(copies, axis, split_axis=0, concat_axis=0, tiled=True)  14.9 us
    ppermute x4, waiting for transfers between devices, extended(): lax.ppermute(lax.slice_in_dim(block, block.shape[dim] - width, None, axis...  11.5 us
    all_to_all x1, starting transfers between devices, from_everyone(): return lax.all_to_all(copies, axis, split_axis=0, concat_axis=0, tiled=True)  11.3 us
    ppermute x4, waiting for transfers between devices, extended(): lax.ppermute(lax.slice_in_dim(block, 0, width, axis=dim), axis, backward)  11 us
    dot_general x27, matrix products, transposed(): jnp.einsum('kc,kyerz->yercz', weights[:, offset], window, preferred_eleme...  10.6 us
    another operation x30, local copies, waits for them, and re-layouts, respond(): jnp.stack([z_padded[shift_y:shift_y + row_count, :, shift_r:shift_r + sli...  10.4 us
  transfers between devices with their start and end apart: 11, of which 7 were waited for; matrix products, arithmetic and copies ran while one was open for 10% of the time, Pallas kernels for 0%

profile of v1, /device:TPU:17, one launch (start us, length us, event | category | flops | bytes accessed | tf_op | source)
XLA Modules:
  0.0 289.1 jit_solution(2482635840673612008)
XLA Ops:
  6.5 0.9 copy.1479
  7.5 2.6 collective-permute-start.1
  10.1 3.4 %collective-permute-start = (bf16[1,1,2,2,192]{4,0,3,2,1:T(2,128)(2,1)S(1)}, bf16[1,1,2,2,192]{4,0,3,2,1:T(2,128)(2,1)S(1)}, u32[]{:S(2)}, u32[]{:S(2)}) collective-permute-start(bf16[1,1,2,2,192]{4,0,3,2,1:T(2,128)(2,1)S(1)} %get-tuple-element.57), channel_id=1, source_target_pairs={{0,2},{2,4},{4,6},{6,8},{8,10},{10,12},{12,14},{14,16},{16,18},{18... | collective-permute-start | bytes 4616 | tf_op jit(solution)/shard_map/ppermute | solution.py:42
  13.5 0.9 copy.1485
  14.6 2.3 collective-permute-start.3
  16.9 1.3 collective-permute-start.2
  18.4 4.6 %collective-permute-done.2 = bf16[26,1,1,2,192]{4,0,3,2,1:T(8,128)(2,1)S(1)} collective-permute-done((bf16[26,1,1,2,192]{4,0,3,2,1:T(8,128)(2,1)S(1)}, bf16[26,1,1,2,192]{4,0,3,2,1:T(8,128)(2,1)S(1)}, u32[]{:S(2)}, u32[]{:S(2)}) %collective-permute-start.2) | collective-permute-done | bytes 20000 | tf_op jit(solution)/shard_map/ppermute | solution.py:42
  25.6 8.0 %stack.141 = bf16[27,24,1,2,2,192]{5,0,4,3,1,2:T(8,128)(2,1)} concatenate(bf16[1,24,1,2,2,192]{5,0,4,3,1,2:T(2,128)(2,1)S(1)} %copy.1401, bf16[1,24,1,2,2,192]{5,0,4,3,1,2:T(2,128)(2,1)S(1)} %copy.1402, bf16[1,24,1,2,2,192]{5,0,4,3,1,2:T(2,128)(2,1)S(1)} %copy.1403, bf16[1,24,1,2,2,192]{5,0,4,3,1,2:T(2,128)(2,1)S(1)} %copy.1404, bf16[1,24,1,2,2,192]{5,0,4,3,1,2:T(2,128)(2,1)S(1)} %copy.1405, ...), dimensions={0} | concatenate | bytes 1990656 | tf_op jit(solution)/shard_map/stack | solution.py:119
  33.6 3.0 %fusion.8 = (bf16[48,24,2,192]{3,0,2,1:T(8,128)(2,1)}, f32[24,2,192,48,1]{2,3,4,1,0:T(8,128)S(1)}) fusion(bf16[48,27,2,1,1]{0,2,1,4,3:T(2,128)(2,1)S(1)} %bitcast.603, bf16[27,24,1,2,2,192]{5,0,4,3,1,2:T(8,128)(2,1)} %stack.141), kind=kOutput, calls=%fused_computation.14 | convolution fusion | flops 48660480 | bytes 3654720 | tf_op jit(solution)/shard_map/koc,oyercz->kyerz/dot_general | solution.py:134
  36.6 1.0 broadcast_in_dim.2
  37.6 11.3 %all-to-all-start = ((bf16[16,24,1,2,2,192]{5,1,4,3,2,0:T(8,128)(2,1)}), bf16[16,24,1,2,2,192]{5,1,4,3,2,0:T(8,128)(2,1)}, u32[]{:S(2)}, u32[]{:S(2)}) async-start(bf16[16,24,1,2,2,192]{5,1,4,3,2,0:T(8,128)(2,1)} %broadcast_in_dim.2), calls=%async_computation | async-start | bytes 1572864 | tf_op jit(solution)/shard_map/all_to_all | solution.py:18
  48.9 1.1 convert_element_type.136
  50.0 0.8 fusion.105
  50.8 0.8 negate_convert_fusion
  51.6 3.3 %multiply_convert_fusion = (bf16[384,384]{1,0:T(8,128)(2,1)}, bf16[384,384]{1,0:T(8,128)(2,1)}) fusion(), kind=kLoop, calls=%fused_computation.144 | loop fusion | flops 1916928 | bytes 589824 | tf_op jit(solution)/shard_map/convert.23
  54.9 1.0 fusion.98
  55.9 0.7 convert_bitcast_fusion
  56.7 14.9 %all-to-all-done = bf16[16,24,1,2,2,192]{5,1,4,3,2,0:T(8,128)(2,1)} async-done(((bf16[16,24,1,2,2,192]{5,1,4,3,2,0:T(8,128)(2,1)}), bf16[16,24,1,2,2,192]{5,1,4,3,2,0:T(8,128)(2,1)}, u32[]{:S(2)}, u32[]{:S(2)}) %all-to-all-start) | async-done | bytes 589856 | tf_op jit(solution)/shard_map/all_to_all | solution.py:18
  71.6 1.3 copy.1390
  72.9 1.3 fusion.120
  74.2 2.2 copy.1469
  76.4 2.2 copy.1468
  78.6 1.4 subtract_convert_fusion.1
  80.1 0.9 copy-done.3
  81.5 0.8 fusion.96
  82.6 0.8 copy-done.4
  83.8 0.8 fusion.95
  85.0 0.9 copy-done.2
  86.4 1.0 add_convert_fusion
  87.4 1.1 copy.1396
  88.5 1.1 copy.1395
  89.8 1.0 copy.1397
  90.8 3.5 %all-to-all-start.1 = ((bf16[16,24,1,2,2,192]{5,1,3,4,2,0:T(8,128)(2,1)}), bf16[16,24,1,2,2,192]{5,1,3,4,2,0:T(8,128)(2,1)S(1)}, u32[]{:S(2)}, u32[]{:S(2)}) async-start(bf16[16,24,1,2,2,192]{5,1,3,4,2,0:T(8,128)(2,1)} %copy.1397), calls=%async_computation.1 | async-start | bytes 1572864 | tf_op jit(solution)/shard_map/all_to_all | solution.py:33
  94.9 21.7 %all-to-all-done.1 = bf16[16,24,1,2,2,192]{5,1,3,4,2,0:T(8,128)(2,1)S(1)} async-done(((bf16[16,24,1,2,2,192]{5,1,3,4,2,0:T(8,128)(2,1)}), bf16[16,24,1,2,2,192]{5,1,3,4,2,0:T(8,128)(2,1)S(1)}, u32[]{:S(2)}, u32[]{:S(2)}) %all-to-all-start.1) | async-done | bytes 589856 | tf_op jit(solution)/shard_map/all_to_all | solution.py:33
  116.7 0.8 convert_reduce_fusion
  117.4 115.2 %all-gather.3.cloned.1.call-done = bf16[384,24,2,192]{3,0,2,1:T(8,128)(2,1)} async-done(((bf16[48,24,2,192]{3,0,2,1:T(8,128)(2,1)}), bf16[384,24,2,192]{3,0,2,1:T(8,128)(2,1)}) %all-gather.3.cloned.1.call-update) | async-done | bytes 7077904 | tf_op jit(solution)/shard_map/all_gather | solution.py:195
  232.7 5.7 %reduce_sum.26 = bf16[48,24,2,192]{3,0,2,1:T(8,128)(2,1)S(1)} reduce(bf16[8,48,24,2,192]{4,1,0,3,2:T(8,128)(2,1)} %bitcast.589, bf16[]{:T(256)} %constant.36.clone.1), dimensions={0}, to_apply=%region_1.2 | reduce | flops 3096576 | bytes 7962626 | tf_op jit(solution)/shard_map/reduce_sum | solution.py:194
  238.4 1.7 fusion.7
  240.0 2.6 collective-permute-start.5
  242.6 3.1 %collective-permute-start.4 = (bf16[48,1,1,2,192]{4,0,3,1,2:T(8,128)(2,1)S(1)}, bf16[48,1,1,2,192]{4,0,3,1,2:T(8,128)(2,1)S(1)}, u32[]{:S(2)}, u32[]{:S(2)}) collective-permute-start(bf16[48,1,1,2,192]{4,0,3,1,2:T(8,128)(2,1)S(1)} %get-tuple-element.23), channel_id=1, source_target_pairs={{0,2},{2,4},{4,6},{6,8},{8,10},{10,12},{12,14},{14,16},{16,18},{18... | collective-permute-start | bytes 110600 | tf_op jit(solution)/shard_map/ppermute | solution.py:42
  245.8 1.1 collective-permute-done.4
  247.2 2.6 collective-permute-start.7
  249.8 1.5 collective-permute-start.6
  252.4 11.0 %collective-permute-done.7 = bf16[48,26,1,1,192]{4,0,3,1,2:T(8,128)(2,1)S(1)} collective-permute-done((bf16[48,26,1,1,192]{4,0,3,1,2:T(8,128)(2,1)S(1)}, bf16[48,26,1,1,192]{4,0,3,1,2:T(8,128)(2,1)S(1)}, u32[]{:S(2)}, u32[]{:S(2)}) %collective-permute-start.7) | collective-permute-done | bytes 479264 | tf_op jit(solution)/shard_map/ppermute | solution.py:45
  263.4 5.7 %collective-permute-done.6 = bf16[48,26,1,1,192]{4,0,3,1,2:T(8,128)(2,1)S(1)} collective-permute-done((bf16[48,26,1,1,192]{4,0,3,1,2:T(8,128)(2,1)S(1)}, bf16[48,26,1,1,192]{4,0,3,1,2:T(8,128)(2,1)S(1)}, u32[]{:S(2)}, u32[]{:S(2)}) %collective-permute-start.6) | collective-permute-done | bytes 479264 | tf_op jit(solution)/shard_map/ppermute | solution.py:42
  269.1 2.4 select_maximum_fusion
  274.2 0.8 pad_maximum_fusion
  281.2 1.1 fusion.87
  (101 shorter events, 15.1 us)
Async XLA Ops:
  6.5 226.1 %all-gather.3.cloned.1.call-start = ((), (), s32[]{:S(2)}) async-start(), calls=%async_computation.2 | async-start | bytes 10616832 | tf_op jit(solution)/shard_map/all_gather | solution.py:195
  7.5 7.0 %collective-permute-start.1 = (bf16[1,1,2,2,192]{4,0,3,2,1:T(2,128)(2,1)S(1)}, bf16[1,1,2,2,192]{4,0,3,2,1:T(2,128)(2,1)S(1)}, u32[]{:S(2)}, u32[]{:S(2)}) collective-permute-start(bf16[1,1,2,2,192]{4,0,3,2,1:T(2,128)(2,1)S(1)} %get-tuple-element.58), channel_id=1, source_target_pairs={{2,0},{4,2},{6,4},{8,6},{10,8},{12,10},{14,12},{16,14},{18,16},{20... | collective-permute-start | bytes 4616 | tf_op jit(solution)/shard_map/ppermute | solution.py:45
  10.1 4.5 %collective-permute-start = (bf16[1,1,2,2,192]{4,0,3,2,1:T(2,128)(2,1)S(1)}, bf16[1,1,2,2,192]{4,0,3,2,1:T(2,128)(2,1)S(1)}, u32[]{:S(2)}, u32[]{:S(2)}) collective-permute-start(bf16[1,1,2,2,192]{4,0,3,2,1:T(2,128)(2,1)S(1)} %get-tuple-element.57), channel_id=1, source_target_pairs={{0,2},{2,4},{4,6},{6,8},{8,10},{10,12},{12,14},{14,16},{16,18},{18... | collective-permute-start | bytes 4616 | tf_op jit(solution)/shard_map/ppermute | solution.py:42
  14.6 3.8 %collective-permute-start.3 = (bf16[26,1,1,2,192]{4,0,3,2,1:T(8,128)(2,1)S(1)}, bf16[26,1,1,2,192]{4,0,3,2,1:T(8,128)(2,1)S(1)}, u32[]{:S(2)}, u32[]{:S(2)}) collective-permute-start(bf16[26,1,1,2,192]{4,0,3,2,1:T(8,128)(2,1)S(1)} %get-tuple-element.52), channel_id=1, source_target_pairs={{1,0},{3,2},{5,4},{7,6},{9,8},{11,10},{13,12},{15,14},{17,16},{19,... | collective-permute-start | bytes 59912 | tf_op jit(solution)/shard_map/ppermute | solution.py:45
  16.9 6.2 %collective-permute-start.2 = (bf16[26,1,1,2,192]{4,0,3,2,1:T(8,128)(2,1)S(1)}, bf16[26,1,1,2,192]{4,0,3,2,1:T(8,128)(2,1)S(1)}, u32[]{:S(2)}, u32[]{:S(2)}) collective-permute-start(bf16[26,1,1,2,192]{4,0,3,2,1:T(8,128)(2,1)S(1)} %get-tuple-element.51), channel_id=1, source_target_pairs={{0,1},{2,3},{4,5},{6,7},{8,9},{10,11},{12,13},{14,15},{16,17},{18,... | collective-permute-start | bytes 59912 | tf_op jit(solution)/shard_map/ppermute | solution.py:42
  25.6 8.0 %copy-start.10 = (bf16[48,3,3,3,2]{0,4,3,2,1:T(2,128)(2,1)S(1)}, bf16[48,3,3,3,2]{0,4,3,2,1:T(2,128)(2,1)}, u32[]{:S(2)}) copy-start(bf16[48,3,3,3,2]{0,4,3,2,1:T(2,128)(2,1)} %param.11) | copy-start | bytes 15556
  33.6 3.0 %copy-start.5 = (f32[24,1,2,2,192]{4,3,2,1,0:T(2,128)S(1)}, f32[24,1,2,2,192]{4,3,2,1,0:T(2,128)}, u32[]{:S(2)}) copy-start(f32[24,1,2,2,192]{4,3,2,1,0:T(2,128)} %param.10) | copy-start | bytes 221188
  37.6 34.0 %all-to-all-start = ((bf16[16,24,1,2,2,192]{5,1,4,3,2,0:T(8,128)(2,1)}), bf16[16,24,1,2,2,192]{5,1,4,3,2,0:T(8,128)(2,1)}, u32[]{:S(2)}, u32[]{:S(2)}) async-start(bf16[16,24,1,2,2,192]{5,1,4,3,2,0:T(8,128)(2,1)} %broadcast_in_dim.2), calls=%async_computation | async-start | bytes 1572864 | tf_op jit(solution)/shard_map/all_to_all | solution.py:18
  50.0 5.9 %copy-start.9 = (s32[384,1,192]{0,2,1:T(8,128)S(1)}, s32[384,1,192]{0,2,1:T(8,128)}, u32[]{:S(2)}) copy-start(s32[384,1,192]{0,2,1:T(8,128)} %param.8) | copy-start | bytes 884740
  80.0 1.0 copy-start.3
  80.0 1.4 copy-start
  80.0 1.4 copy-start.1
  82.5 1.0 copy-start.4
  82.5 1.2 copy-start.7
  84.9 1.0 copy-start.2
  90.8 25.9 %all-to-all-start.1 = ((bf16[16,24,1,2,2,192]{5,1,3,4,2,0:T(8,128)(2,1)}), bf16[16,24,1,2,2,192]{5,1,3,4,2,0:T(8,128)(2,1)S(1)}, u32[]{:S(2)}, u32[]{:S(2)}) async-start(bf16[16,24,1,2,2,192]{5,1,3,4,2,0:T(8,128)(2,1)} %copy.1397), calls=%async_computation.1 | async-start | bytes 1572864 | tf_op jit(solution)/shard_map/all_to_all | solution.py:33
  238.3 7.4 %copy-start.8 = (f32[24,2,2,192]{3,0,1,2:T(8,128)S(1)}, f32[24,2,2,192]{3,0,1,2:T(8,128)}, u32[]{:S(2)}) copy-start(f32[24,2,2,192]{3,0,1,2:T(8,128)} %convert_reduce_fusion) | copy-start | bytes 221188
  240.0 5.7 %collective-permute-start.5 = (bf16[48,1,1,2,192]{4,0,3,1,2:T(8,128)(2,1)S(1)}, bf16[48,1,1,2,192]{4,0,3,1,2:T(8,128)(2,1)S(1)}, u32[]{:S(2)}, u32[]{:S(2)}) collective-permute-start(bf16[48,1,1,2,192]{4,0,3,1,2:T(8,128)(2,1)S(1)} %get-tuple-element.24), channel_id=1, source_target_pairs={{2,0},{4,2},{6,4},{8,6},{10,8},{12,10},{14,12},{16,14},{18,16},{20... | collective-permute-start | bytes 110600 | tf_op jit(solution)/shard_map/ppermute | solution.py:45
  242.6 4.3 %collective-permute-start.4 = (bf16[48,1,1,2,192]{4,0,3,1,2:T(8,128)(2,1)S(1)}, bf16[48,1,1,2,192]{4,0,3,1,2:T(8,128)(2,1)S(1)}, u32[]{:S(2)}, u32[]{:S(2)}) collective-permute-start(bf16[48,1,1,2,192]{4,0,3,1,2:T(8,128)(2,1)S(1)} %get-tuple-element.23), channel_id=1, source_target_pairs={{0,2},{2,4},{4,6},{6,8},{8,10},{10,12},{12,14},{14,16},{16,18},{18... | collective-permute-start | bytes 110600 | tf_op jit(solution)/shard_map/ppermute | solution.py:42
  247.2 16.2 %collective-permute-start.7 = (bf16[48,26,1,1,192]{4,0,3,1,2:T(8,128)(2,1)S(1)}, bf16[48,26,1,1,192]{4,0,3,1,2:T(8,128)(2,1)S(1)}, u32[]{:S(2)}, u32[]{:S(2)}) collective-permute-start(bf16[48,26,1,1,192]{4,0,3,1,2:T(8,128)(2,1)S(1)} %get-tuple-element.22), channel_id=1, source_target_pairs={{1,0},{3,2},{5,4},{7,6},{9,8},{11,10},{13,12},{15,14},{17,16},{19,... | collective-permute-start | bytes 1437704 | tf_op jit(solution)/shard_map/ppermute | solution.py:45
  249.8 19.3 %collective-permute-start.6 = (bf16[48,26,1,1,192]{4,0,3,1,2:T(8,128)(2,1)S(1)}, bf16[48,26,1,1,192]{4,0,3,1,2:T(8,128)(2,1)S(1)}, u32[]{:S(2)}, u32[]{:S(2)}) collective-permute-start(bf16[48,26,1,1,192]{4,0,3,1,2:T(8,128)(2,1)S(1)} %get-tuple-element.21), channel_id=1, source_target_pairs={{0,1},{2,3},{4,5},{6,7},{8,9},{10,11},{12,13},{14,15},{16,17},{18,... | collective-permute-start | bytes 1437704 | tf_op jit(solution)/shard_map/ppermute | solution.py:42
  280.3 0.9 copy-start.6
Sparse Core Ops, SparseCore 0:
  36.7 195.8 all-gather.2
